TPU v7x, 128 devices: a whole 4x4x4 slice. The times are simulated.
128 devices in a mesh: ctx: 64 (over z, x, y), wsh: 2 (over core).
Axes of the slice: x: 4, y: 4, z: 4, core: 2. Of those that a mesh axis runs over, the one named last changes fastest.
Arguments:
- block_input: bfloat16 [2, 8192, 640], P('wsh', 'ctx'), may hold values from -6 to 6
- cotangent: float32 [2, 8192, 640], P('wsh', 'ctx'), may hold values from -6 to 6
- pair_blocks: int32 [64, 2], replicated, may hold values from 0 to 127, as said below
- w_query: bfloat16 [640, 1024], P(None, 'wsh'), may hold values from -0.25 to 0.25
- w_key: bfloat16 [640, 256], P(None, 'wsh'), may hold values from -0.25 to 0.25
- w_value: bfloat16 [640, 256], P(None, 'wsh'), may hold values from -0.25 to 0.25
- w_out: bfloat16 [1024, 640], P('wsh'), may hold values from -0.1875 to 0.1875
- w_gate: bfloat16 [640, 2048], P(None, 'wsh'), may hold values from -0.25 to 0.25
- w_up: bfloat16 [640, 2048], P(None, 'wsh'), may hold values from -0.25 to 0.25
- w_down: bfloat16 [2048, 640], P('wsh'), may hold values from -0.125 to 0.125
- attn_pre_gain: bfloat16 [640], P('wsh'), may hold values from -0.3984375 to 0.59765625
- query_gain: bfloat16 [256], P('wsh'), may hold values from -0.3984375 to 0.59765625
- key_gain: bfloat16 [256], P('wsh'), may hold values from -0.3984375 to 0.59765625
- attn_post_gain: bfloat16 [640], P('wsh'), may hold values from -0.3984375 to 0.59765625
- ffw_pre_gain: bfloat16 [640], P('wsh'), may hold values from -0.3984375 to 0.59765625
- ffw_post_gain: bfloat16 [640], P('wsh'), may hold values from -0.3984375 to 0.59765625
Outputs:
- block_output: float32 [2, 8192, 640], P('wsh', 'ctx')
- input_grad: float32 [2, 8192, 640], P('wsh', 'ctx')
- w_query_grad: float32 [640, 1024], P(None, 'wsh')
- w_key_grad: float32 [640, 256], P(None, 'wsh')
- w_value_grad: float32 [640, 256], P(None, 'wsh')
- w_out_grad: float32 [1024, 640], P('wsh')
- w_gate_grad: float32 [640, 2048], P(None, 'wsh')
- w_up_grad: float32 [640, 2048], P(None, 'wsh')
- w_down_grad: float32 [2048, 640], P('wsh')
- attn_pre_gain_grad: float32 [640], P('wsh')
- query_gain_grad: float32 [256], P('wsh')
- key_gain_grad: float32 [256], P('wsh')
- attn_post_gain_grad: float32 [640], P('wsh')
- ffw_pre_gain_grad: float32 [640], P('wsh')
- ffw_post_gain_grad: float32 [640], P('wsh')
Inputs may be any that keep to these rules, and one draw needn't show every extreme that they name: `pair_blocks`: row r holds a block b and its mirror 2 * 64 - 1 - b, in the order in which index r of ctx stores them; over all rows every one of the 128 blocks appears exactly once.
All inputs are finite; a program needn't handle non-finite values.
Results may differ from a plain program's by a relative error of at most 0.018.
Values may be sent and summed in bfloat16 or wider, within the bound.
No kernel may reach another device: no remote copies, remote signals or barrier semaphores. Data moves between devices by JAX's collectives and lax.ppermute only.
A program may use at most 192 MiB of HBM per device.

v0:
```python
import jax
import jax.numpy as jnp
from jax import lax
from jax.sharding import Mesh
from jax.sharding import PartitionSpec as P

HEADS = 4
HDIM = 256
CTX = ("z", "x", "y")
epsilon = 1e-06
theta_base = 1000000.0
bf16 = jnp.bfloat16
f32 = jnp.float32


def rms_forward(values, gain_w):
    factor = lax.rsqrt(jnp.mean(values * values, axis=-1, keepdims=True) + epsilon)
    return (values * factor * (1.0 + gain_w), factor)


def rms_backward(values, factor, gain_w, grad_out):
    weighted = grad_out * (1.0 + gain_w)
    inner = jnp.mean(weighted * values, axis=-1, keepdims=True)
    grad_in = factor * (weighted - values * factor * factor * inner)
    grad_gain = jnp.sum((grad_out * values * factor).reshape(-1, values.shape[-1]), axis=0)
    return (grad_in, grad_gain)


def rotary_tables(positions, width):
    half_width = width // 2
    frequency = theta_base ** (-jnp.arange(half_width, dtype=f32) * 2.0 / width)
    angles = positions.astype(f32)[:, None] * frequency[None, :]
    return (jnp.cos(angles), jnp.sin(angles))


def rotate(values, cos_tab, sin_tab):
    half = values.shape[-1] // 2
    a, b = (values[..., :half], values[..., half:])
    return jnp.concatenate([a * cos_tab - b * sin_tab, b * cos_tab + a * sin_tab], axis=-1)


def rotate_back(grads, cos_tab, sin_tab):
    half = grads.shape[-1] // 2
    a, b = (grads[..., :half], grads[..., half:])
    return jnp.concatenate([a * cos_tab + b * sin_tab, b * cos_tab - a * sin_tab], axis=-1)


def block_positions(block_ids, half_rows):
    offsets = jnp.arange(half_rows, dtype=jnp.int32)
    return (block_ids[:, None] * half_rows + offsets[None, :]).reshape(-1)


def dot_f32(left, right):
    return jnp.dot(left, right, preferred_element_type=f32)


def dot_nt(left, right):
    return lax.dot_general(left, right, (((1,), (1,)), ((), ())), preferred_element_type=f32)


def dot_tn(left, right):
    return lax.dot_general(left, right, (((0,), (0,)), ((), ())), preferred_element_type=f32)


def swap(values):
    return lax.ppermute(values, "wsh", [(0, 1), (1, 0)])


def attention_forward(query, keys, vals, query_pos, key_pos):
    scores = dot_nt(query, keys) * HDIM ** (-0.5)
    scores = jnp.where(key_pos[None, :] <= query_pos[:, None], scores, -1e30)
    top = jnp.max(scores, axis=-1, keepdims=True)
    shifted = jnp.exp(scores - top)
    totals = jnp.sum(shifted, axis=-1, keepdims=True)
    probs = (shifted / totals).astype(bf16)
    return (dot_f32(probs, vals).astype(bf16), top + jnp.log(totals))


def attention_backward(query, keys, vals, query_pos, key_pos, grads, log_total, delta):
    scores = dot_nt(query, keys) * HDIM ** (-0.5)
    scores = jnp.where(key_pos[None, :] <= query_pos[:, None], scores, -1e30)
    probs = jnp.exp(scores - log_total)
    grad_probs = dot_nt(grads, vals)
    grad_scores = (probs * (grad_probs - delta)).astype(bf16)
    grad_query = dot_f32(grad_scores, keys) * HDIM ** (-0.5)
    grad_key = dot_tn(grad_scores, query) * HDIM ** (-0.5)
    grad_value = dot_tn(probs.astype(bf16), grads)
    return (grad_query, jnp.concatenate([grad_key.astype(bf16), grad_value.astype(bf16)], axis=1))


def gather_ctx(block):
    return lax.all_gather(block, CTX, axis=0, tiled=True)


def scatter_sum(parts):
    got = lax.all_to_all(parts.reshape(64, 128, -1), CTX, split_axis=0, concat_axis=0, tiled=True)
    return jnp.sum(got.astype(f32), axis=0)


def small_sum(values):
    rows = values.shape[0] // 64
    got = lax.all_to_all(values.reshape(64, rows, -1), CTX, split_axis=0, concat_axis=0, tiled=True)
    mine = jnp.sum(got.astype(f32), axis=0).astype(values.dtype)
    wide = jnp.broadcast_to(mine[None], (64,) + mine.shape)
    out = lax.all_to_all(wide, CTX, split_axis=0, concat_axis=0, tiled=True)
    return out.reshape(values.shape)


def per_device(
    block_input,
    cotangent,
    pair_blocks,
    w_query,
    w_key,
    w_value,
    w_out,
    w_gate,
    w_up,
    w_down,
    attn_pre_gain,
    query_gain,
    key_gain,
    attn_post_gain,
    ffw_pre_gain,
    ffw_post_gain,
):
    rows = block_input.shape[1]
    rank = lax.axis_index(CTX)
    first = lax.axis_index("wsh") == 0

    def ordered(own, other, axis):
        return jnp.where(
            first,
            jnp.concatenate([own, other], axis=axis),
            jnp.concatenate([other, own], axis=axis),
        )

    resid_in = block_input[0].astype(f32)
    grad_top = cotangent[0]
    query_pos = block_positions(lax.dynamic_slice_in_dim(pair_blocks, rank, 1, 0)[0], rows // 2)
    key_pos = block_positions(pair_blocks.reshape(-1), rows // 2)
    cos_tab, sin_tab = rotary_tables(query_pos, HDIM)
    gains_own = jnp.concatenate(
        [attn_pre_gain, attn_post_gain, ffw_pre_gain, ffw_post_gain, query_gain, key_gain]
    )[None]
    gains_other = swap(gains_own)
    kv_own = jnp.concatenate([w_key, w_value], axis=1)
    kv_other = swap(kv_own)

    def gain(start, width):
        return ordered(
            gains_own[0, start : start + width], gains_other[0, start : start + width], 0
        ).astype(f32)[None]

    gain_one, gain_two, gain_three, gain_four = (gain(320 * i, 320) for i in range(4))
    gain_query, gain_key = (gain(1280, 128), gain(1408, 128))
    key_w = ordered(kv_own[:, :128], kv_other[:, :128], 1)
    value_w = ordered(kv_own[:, 128:], kv_other[:, 128:], 1)
    normed_one, factor_one = rms_forward(resid_in, gain_one)
    attn_in = normed_one.astype(bf16)
    key_raw = dot_f32(attn_in, key_w)
    value_bf = dot_f32(attn_in, value_w).astype(bf16)
    key_normed, key_factor = rms_forward(key_raw, gain_key)
    key_rot = rotate(key_normed, cos_tab, sin_tab).astype(bf16)
    kv_all = gather_ctx(jnp.concatenate([key_rot, value_bf], axis=1))
    key_all, value_all = (kv_all[:, :HDIM], kv_all[:, HDIM:])
    query_w = (w_query, swap(w_query))
    out_w = (w_out, swap(w_out))
    gate_w = (w_gate, swap(w_gate))
    up_w = (w_up, swap(w_up))
    down_w = (w_down, swap(w_down))

    def heads_first(pair):
        return jnp.concatenate(
            [half[:, HDIM * h : HDIM * (h + 1)] for half in pair for h in range(2)], axis=0
        )

    def heads_last(stacked):
        return tuple(
            (
                jnp.concatenate(
                    [stacked[rows * h : rows * (h + 1)] for h in (2 * p, 2 * p + 1)], axis=1
                )
                for p in range(2)
            )
        )

    cos4, sin4 = (jnp.tile(cos_tab, (HEADS, 1)), jnp.tile(sin_tab, (HEADS, 1)))
    query_raw = heads_first(tuple((dot_f32(attn_in, half) for half in query_w)))
    query_normed, query_factor = rms_forward(query_raw, gain_query)
    query_rot = rotate(query_normed, cos4, sin4).astype(bf16)
    pos4 = jnp.tile(query_pos, HEADS)
    attn_heads, log_total = attention_forward(query_rot, key_all, value_all, pos4, key_pos)
    attn_out = heads_last(attn_heads)
    attn_proj = dot_f32(attn_out[0], out_w[0]) + dot_f32(attn_out[1], out_w[1])
    normed_two, factor_two = rms_forward(attn_proj, gain_two)
    mid = resid_in + normed_two
    normed_three, factor_three = rms_forward(mid, gain_three)
    ffw_in = normed_three.astype(bf16)
    gate = [dot_f32(ffw_in, half) for half in gate_w]
    up_val = [dot_f32(ffw_in, half) for half in up_w]
    acts = [jax.vjp(lambda inner: jax.nn.gelu(inner, approximate=True), g) for g in gate]
    hidden = [(act[0] * up).astype(bf16) for act, up in zip(acts, up_val)]
    ffw_proj = dot_f32(hidden[0], down_w[0]) + dot_f32(hidden[1], down_w[1])
    normed_four, factor_four = rms_forward(ffw_proj, gain_four)
    block_output = mid + normed_four
    grad_ffw, grad_gain_four = rms_backward(ffw_proj, factor_four, gain_four, grad_top)
    grad_ffw_bf = grad_ffw.astype(bf16)
    grad_hidden = [dot_nt(grad_ffw_bf, half) for half in down_w]
    grad_gate = [act[1](gh * up)[0].astype(bf16) for act, gh, up in zip(acts, grad_hidden, up_val)]
    grad_up = [(gh * act[0]).astype(bf16) for act, gh in zip(acts, grad_hidden)]
    grad_ffw_in = (
        dot_nt(grad_gate[0], gate_w[0])
        + dot_nt(grad_gate[1], gate_w[1])
        + dot_nt(grad_up[0], up_w[0])
        + dot_nt(grad_up[1], up_w[1])
    )
    grad_mid_part, grad_gain_three = rms_backward(mid, factor_three, gain_three, grad_ffw_in)
    grad_mid = grad_top + grad_mid_part
    grad_proj, grad_gain_two = rms_backward(attn_proj, factor_two, gain_two, grad_mid)
    grad_proj_bf = grad_proj.astype(bf16)
    grad_attn = tuple((dot_nt(grad_proj_bf, half).astype(bf16) for half in out_w))
    grad_heads = heads_first(grad_attn)

    def both(own, other):
        return jnp.concatenate([own, swap(other)], axis=0)

    ffw_in2 = both(ffw_in, ffw_in)
    grad_w_down = dot_tn(both(hidden[0], hidden[1]), both(grad_ffw_bf, grad_ffw_bf))
    grad_w_gate = dot_tn(ffw_in2, both(grad_gate[0], grad_gate[1]))
    grad_w_up = dot_tn(ffw_in2, both(grad_up[0], grad_up[1]))
    grad_w_out = dot_tn(both(attn_out[0], attn_out[1]), both(grad_proj_bf, grad_proj_bf))
    attn_in2 = both(attn_in, attn_in)
    delta = jnp.sum(grad_heads.astype(f32) * attn_heads.astype(f32), axis=-1, keepdims=True)
    grad_query, kv_terms = attention_backward(
        query_rot, key_all, value_all, pos4, key_pos, grad_heads, log_total, delta
    )
    grad_query_raw, grad_gain_query = rms_backward(
        query_raw, query_factor, gain_query, rotate_back(grad_query, cos4, sin4)
    )
    grad_query_bf = heads_last(grad_query_raw.astype(bf16))
    grad_w_query = dot_tn(attn_in2, both(grad_query_bf[0], grad_query_bf[1]))
    big = tuple(
        (g.astype(bf16) for g in (grad_w_query, grad_w_out, grad_w_gate, grad_w_up, grad_w_down))
    )
    sum_query, sum_out, sum_gate, sum_up, sum_down = (g.astype(f32) for g in lax.psum(big, CTX))
    kv_mine = scatter_sum(kv_terms)
    grad_key_raw, grad_gain_key = rms_backward(
        key_raw, key_factor, gain_key, rotate_back(kv_mine[:, :HDIM], cos_tab, sin_tab)
    )
    grad_key_bf = grad_key_raw.astype(bf16)
    grad_value_bf = kv_mine[:, HDIM:].astype(bf16)

    def mine_other(full):
        a, b = (full[:, :128], full[:, 128:])
        return (jnp.where(first, a, b), jnp.where(first, b, a))

    key_m, key_o = mine_other(grad_key_bf)
    val_m, val_o = mine_other(grad_value_bf)
    grad_kv2 = both(
        jnp.concatenate([key_m, val_m], axis=1), jnp.concatenate([key_o, val_o], axis=1)
    )
    grad_w_kv = dot_tn(grad_kv2, attn_in2)
    grad_attn_in = (
        dot_nt(grad_query_bf[0], query_w[0])
        + dot_nt(grad_query_bf[1], query_w[1])
        + dot_nt(grad_key_bf, key_w)
        + dot_nt(grad_value_bf, value_w)
    )
    grad_in_part, grad_gain_one = rms_backward(resid_in, factor_one, gain_one, grad_attn_in)
    input_grad = grad_mid + grad_in_part
    gain_grads = (
        grad_gain_one,
        grad_gain_two,
        grad_gain_three,
        grad_gain_four,
        grad_gain_query,
        grad_gain_key,
    )
    g_own = jnp.concatenate(
        [jnp.where(first, g[: g.size // 2], g[g.size // 2 :]) for g in gain_grads]
    )
    g_other = jnp.concatenate(
        [jnp.where(first, g[g.size // 2 :], g[: g.size // 2]) for g in gain_grads]
    )
    g_sum = g_own + swap(g_other[None])[0]
    g_block = jnp.concatenate([g_sum, jnp.zeros((1024,), f32)]).reshape(64, 40).astype(bf16)
    late = jnp.concatenate([grad_w_kv.astype(bf16).reshape(64, 2560), g_block], axis=1)
    late = small_sum(late).astype(f32)
    sum_kv = late[:, :2560].reshape(256, 640)
    sum_gains = late[:, 2560:].reshape(-1)
    return (
        block_output[None],
        input_grad[None],
        sum_query,
        sum_kv[:128].T,
        sum_kv[128:].T,
        sum_out,
        sum_gate,
        sum_up,
        sum_down,
        sum_gains[:320],
        sum_gains[1280:1408],
        sum_gains[1408:1536],
        sum_gains[320:640],
        sum_gains[640:960],
        sum_gains[960:1280],
    )


def solution(mesh):
    grid = Mesh(mesh.devices.reshape(4, 4, 4, 2), ("z", "x", "y", "wsh"))
    tokens = P("wsh", CTX, None)
    cols, rows, vec = (P(None, "wsh"), P("wsh", None), P("wsh"))
    return jax.shard_map(
        per_device,
        mesh=grid,
        in_specs=(tokens, tokens, P(), cols, cols, cols, rows, cols, cols, rows) + (vec,) * 6,
        out_specs=(tokens, tokens, cols, cols, cols, rows, cols, cols, rows) + (vec,) * 6,
        check_vma=False,
    )
```

profile of v0, /device:TPU:0, one launch (start us, length us, event | category | flops | bytes accessed | tf_op | source)
XLA Modules:
  0.0 476.8 jit_solution(2237025595340672218)
XLA Ops:
  7.2 4.3 concatenate.211
  26.4 75.5 %all-gather.2.cloned.1.call-done = bf16[8192,512]{1,0:T(8,128)(2,1)} async-done(((bf16[128,512]{1,0:T(8,128)(2,1)}), bf16[8192,512]{1,0:T(8,128)(2,1)}) %all-gather.2.cloned.1.call-update) | async-done | bytes 8388624 | tf_op jit(solution)/shard_map/all_gather | solution.py:92
  101.9 10.8 %fusion.133 = (f32[512]{0:T(512)S(1)}, f32[512,8192]{1,0:T(8,128)}) fusion(bf16[8192,512]{1,0:T(8,128)(2,1)} %all-gather.2.cloned.1.call-done, bf16[512,128]{1,0:T(8,128)(2,1)} %get-tuple-element.99, bf16[512,128]{1,0:T(8,128)(2,1)S(1)} %get-tuple-element.98, s32[512]{0:T(512)S(1)} %broadcast_bitcast_fusion, s32[8192]{0:T(1024)S(1)} %add.247), kind=kOutput, calls=%fused_computation.278 | convolution fusion | flops 2164784640 | bytes 21270528 | tf_op jit(solution)/shard_map/dot_general | solution.py:58
  112.8 8.1 %fusion = f32[512]{0:T(512)S(1)} fusion(f32[512,8192]{1,0:T(8,128)} %get-tuple-element.159, f32[512]{0:T(512)S(1)} %get-tuple-element.158), kind=kLoop, calls=%fused_computation.6 | loop fusion | flops 8388096 | bytes 16781312 | tf_op jit(solution)/shard_map/reduce_sum | solution.py:74
  120.9 10.0 %fusion.14 = bf16[512,256]{0,1:T(8,128)(2,1)S(1)} fusion(bf16[8192,512]{1,0:T(8,128)(2,1)} %all-gather.2.cloned.1.call-done, f32[512,8192]{1,0:T(8,128)} %get-tuple-element.159, f32[512]{0:T(512)S(1)} %fusion, f32[512]{0:T(512)S(1)} %get-tuple-element.158), kind=kOutput, calls=%fused_computation.27 | convolution fusion | flops 2160197632 | bytes 21237760 | tf_op jit(solution)/shard_map/dot_general | solution.py:54
  134.4 1.7 fusion.136
  137.0 1.8 fusion.138
  139.3 1.9 multiply_reduce_fusion.9
  143.6 2.0 fusion.139
  145.7 2.2 multiply_convert_fusion.2
  147.9 2.1 convolution_add_fusion.5
  156.1 5.2 %convolution_convert_fusion = bf16[8192,256]{0,1:T(8,128)(2,1)} fusion(f32[512,8192]{1,0:T(8,128)S(1)} %bitcast.112, f32[512]{0:T(512)S(1)} %log_add_fusion, bf16[128,256]{0,1:T(8,128)(2,1)S(1)} %get-tuple-element.131, bf16[128,256]{0,1:T(8,128)(2,1)S(1)} %get-tuple-element.130, bf16[128,256]{0,1:T(8,128)(2,1)} %copy-done.20, bf16[128,256]{0,1:T(8,128)(2,1)} %copy-done.19), kind=kOutput, calls=%fused_computation.8 | convolution fusion | flops 2159017984 | bytes 21235712 | tf_op jit(solution)/shard_map/dot_general | solution.py:62
  161.3 10.0 %multiply_convert_fusion = bf16[512,8192]{1,0:T(8,128)(2,1)S(1)} fusion(f32[512,8192]{1,0:T(8,128)} %get-tuple-element.159, f32[512]{0:T(512)S(1)} %multiply_reduce_fusion.2, f32[512]{0:T(512)S(1)} %log_add_fusion, bf16[8192,512]{1,0:T(8,128)(2,1)} %all-gather.2.cloned.1.call-done, bf16[128,256]{0,1:T(8,128)(2,1)S(1)} %get-tuple-element.131, ...), kind=kOutput, calls=%fused_computation.1 | convolution fusion | flops 2165309440 | bytes 29626368 | tf_op jit(solution)/shard_map/dot_general | solution.py:58
  171.3 2.4 fusion.2
  173.7 1.8 copy-done.1
  176.6 4.4 copy_bitcast_fusion
  181.0 9.0 %all-to-all-start = ((bf16[64,128,512]{1,2,0:T(8,128)(2,1)}), bf16[64,128,512]{1,2,0:T(8,128)(2,1)}, u32[]{:S(2)}, u32[]{:S(2)}) async-start(bf16[64,128,512]{1,2,0:T(8,128)(2,1)} %copy_bitcast_fusion), calls=%async_computation | async-start | bytes 16777216 | tf_op jit(solution)/shard_map/all_to_all | solution.py:96
  190.2 6.9 %fusion.11 = f32[512,256]{1,0:T(8,128)S(1)} fusion(bf16[512,8192]{1,0:T(8,128)(2,1)} %copy-done.1, bf16[8192,512]{1,0:T(8,128)(2,1)} %all-gather.2.cloned.1.call-done), kind=kOutput, calls=%fused_computation.26 | convolution fusion | flops 2147614720 | bytes 13107200 | tf_op jit(solution)/shard_map/dot_general | solution.py:54
  203.0 1.6 convolution_convert_fusion.3
  206.2 1.7 convolution_convert_fusion.1
  211.0 97.9 %all-to-all-done = bf16[64,128,512]{1,2,0:T(8,128)(2,1)} async-done(((bf16[64,128,512]{1,2,0:T(8,128)(2,1)}), bf16[64,128,512]{1,2,0:T(8,128)(2,1)}, u32[]{:S(2)}, u32[]{:S(2)}) %all-to-all-start) | async-done | bytes 8388640 | tf_op jit(solution)/shard_map/all_to_all | solution.py:96
  308.9 4.8 convert_reduce_fusion
  319.9 8.7 %all-to-all-start.1 = ((bf16[64,2,1300]{2,1,0:T(2,128)(2,1)}), bf16[64,2,1300]{2,1,0:T(2,128)(2,1)S(1)}, u32[]{:S(2)}, u32[]{:S(2)}) async-start(bf16[64,2,1300]{2,1,0:T(2,128)(2,1)} %reshape.477), calls=%async_computation.1 | async-start | bytes 720896 | tf_op jit(solution)/shard_map/all_to_all | solution.py:102
  328.7 100.5 %all-reduce.4.cloned.1.call-done = (bf16[640,512]{1,0:T(8,128)(2,1)}, bf16[512,640]{1,0:T(8,128)(2,1)}, bf16[640,1024]{1,0:T(8,128)(2,1)}, bf16[640,1024]{1,0:T(8,128)(2,1)}, bf16[1024,640]{1,0:T(8,128)(2,1)}) async-done(((bf16[640,512]{1,0:T(8,128)(2,1)}, bf16[512,640]{1,0:T(8,128)(2,1)}, bf16[640,1024]{1,0:T(8,128)(2,1)}, bf16[640,1024]{1,0:T(8,128)(2,1)}, bf16[1024,640]{1,0:T(8,128)(2,1)}), ...) | async-done | bytes 5242896 | tf_op jit(solution)/shard_map/psum | solution.py:246
  429.2 2.5 convert_element_type.209
  431.7 2.2 convert_element_type.215
  433.9 1.8 convert_element_type.217
  435.7 1.8 convert_element_type.219
  437.5 1.7 convert_element_type.221
  440.7 2.8 reduce.22
  444.6 7.7 %all-to-all-start.2 = ((bf16[64,2,1300]{2,1,0:T(2,128)(2,1)}), bf16[64,2,1300]{2,1,0:T(2,128)(2,1)S(1)}, u32[]{:S(2)}, u32[]{:S(2)}) async-start(bf16[64,2,1300]{2,1,0:T(2,128)(2,1)} %reshape.479), calls=%async_computation.2 | async-start | bytes 720896 | tf_op jit(solution)/shard_map/all_to_all | solution.py:105
  453.2 10.7 %all-to-all-done.2 = bf16[64,2,1300]{2,1,0:T(2,128)(2,1)S(1)} async-done(((bf16[64,2,1300]{2,1,0:T(2,128)(2,1)}), bf16[64,2,1300]{2,1,0:T(2,128)(2,1)S(1)}, u32[]{:S(2)}, u32[]{:S(2)}) %all-to-all-start.2) | async-done | bytes 332832 | tf_op jit(solution)/shard_map/all_to_all | solution.py:105
  (323 shorter events, 54.3 us)
Async XLA Ops:
  7.2 94.7 %all-gather.2.cloned.1.call-start = ((), (), s32[]{:S(2)}) async-start(), calls=%async_computation.3 | async-start | bytes 8519680 | tf_op jit(solution)/shard_map/all_gather | solution.py:92
  11.5 3.9 collective-permute-start
  12.7 4.0 collective-permute-start.2
  20.6 3.4 collective-permute-start.1
  20.7 111.9 %collective-permute-start.3 = (bf16[512,640]{1,0:T(8,128)(2,1)}, bf16[512,640]{1,0:T(8,128)(2,1)}, u32[]{:S(2)}, u32[]{:S(2)}) collective-permute-start(bf16[512,640]{1,0:T(8,128)(2,1)} %param.22), channel_id=1, source_target_pairs={{0,1},{1,0},{2,3},{3,2},{4,5},{5,4},{6,7},{7,6},{8,9},{9,8},{10,11... | collective-permute-start | bytes 1966088 | tf_op jit(solution)/shard_map/ppermute | solution.py:66
  21.2 115.8 %collective-permute-start.4 = (bf16[640,1024]{1,0:T(8,128)(2,1)}, bf16[640,1024]{1,0:T(8,128)(2,1)}, u32[]{:S(2)}, u32[]{:S(2)}) collective-permute-start(bf16[640,1024]{1,0:T(8,128)(2,1)} %param.23), channel_id=1, source_target_pairs={{0,1},{1,0},{2,3},{3,2},{4,5},{5,4},{6,7},{7,6},{8,9},{9,8},{10,11... | collective-permute-start | bytes 3932168 | tf_op jit(solution)/shard_map/ppermute | solution.py:66
  21.4 117.5 %collective-permute-start.5 = (bf16[640,1024]{1,0:T(8,128)(2,1)S(1)}, bf16[640,1024]{1,0:T(8,128)(2,1)S(1)}, u32[]{:S(2)}, u32[]{:S(2)}) collective-permute-start(bf16[640,1024]{1,0:T(8,128)(2,1)S(1)} %copy-done.2), channel_id=1, source_target_pairs={{0,1},{1,0},{2,3},{3,2},{4,5},{5,4},{6,7},{7,6},{8,9},{9,8},{10,11... | collective-permute-start | bytes 3932168 | tf_op jit(solution)/shard_map/ppermute | solution.py:66
  21.8 117.5 %collective-permute-start.6 = (bf16[1024,640]{1,0:T(8,128)(2,1)}, bf16[1024,640]{1,0:T(8,128)(2,1)}, u32[]{:S(2)}, u32[]{:S(2)}) collective-permute-start(bf16[1024,640]{1,0:T(8,128)(2,1)} %param.25), channel_id=1, source_target_pairs={{0,1},{1,0},{2,3},{3,2},{4,5},{5,4},{6,7},{7,6},{8,9},{9,8},{10,11... | collective-permute-start | bytes 3932168 | tf_op jit(solution)/shard_map/ppermute | solution.py:66
  181.0 127.9 %all-to-all-start = ((bf16[64,128,512]{1,2,0:T(8,128)(2,1)}), bf16[64,128,512]{1,2,0:T(8,128)(2,1)}, u32[]{:S(2)}, u32[]{:S(2)}) async-start(bf16[64,128,512]{1,2,0:T(8,128)(2,1)} %copy_bitcast_fusion), calls=%async_computation | async-start | bytes 16777216 | tf_op jit(solution)/shard_map/all_to_all | solution.py:96
  190.0 239.2 %all-reduce.4.cloned.1.call-start = ((), (), s32[]{:S(2)}) async-start(), calls=%async_computation.4 | async-start | bytes 10485760 | tf_op jit(solution)/shard_map/psum | solution.py:246
  190.1 9.1 %collective-permute-start.7 = (bf16[128,640]{1,0:T(8,128)(2,1)S(1)}, bf16[128,640]{1,0:T(8,128)(2,1)S(1)}, u32[]{:S(2)}, u32[]{:S(2)}) collective-permute-start(bf16[128,640]{1,0:T(8,128)(2,1)S(1)} %copy-done.10), channel_id=1, source_target_pairs={{0,1},{1,0},{2,3},{3,2},{4,5},{5,4},{6,7},{7,6},{8,9},{9,8},{10,11... | collective-permute-start | bytes 491528 | tf_op jit(solution)/shard_map/ppermute | solution.py:66
  197.9 1.7 collective-permute-start.8
  198.5 2.9 collective-permute-start.12
  198.6 4.4 collective-permute-start.14
  199.0 2.0 collective-permute-start.11
  199.2 3.8 collective-permute-start.13
  199.6 4.9 %collective-permute-start.15 = (bf16[128,1024]{1,0:T(8,128)(2,1)S(1)}, bf16[128,1024]{1,0:T(8,128)(2,1)S(1)}, u32[]{:S(2)}, u32[]{:S(2)}) collective-permute-start(bf16[128,1024]{1,0:T(8,128)(2,1)S(1)} %copy-done.38), channel_id=1, source_target_pairs={{0,1},{1,0},{2,3},{3,2},{4,5},{5,4},{6,7},{7,6},{8,9},{9,8},{10,11... | collective-permute-start | bytes 786440 | tf_op jit(solution)/shard_map/ppermute | solution.py:66
  201.1 5.1 %collective-permute-start.16 = (bf16[128,1024]{1,0:T(8,128)(2,1)S(1)}, bf16[128,1024]{1,0:T(8,128)(2,1)S(1)}, u32[]{:S(2)}, u32[]{:S(2)}) collective-permute-start(bf16[128,1024]{1,0:T(8,128)(2,1)S(1)} %copy-done.24), channel_id=1, source_target_pairs={{0,1},{1,0},{2,3},{3,2},{4,5},{5,4},{6,7},{7,6},{8,9},{9,8},{10,11... | collective-permute-start | bytes 786440 | tf_op jit(solution)/shard_map/ppermute | solution.py:66
  201.4 4.8 %collective-permute-start.17 = (bf16[128,640]{1,0:T(8,128)(2,1)S(1)}, bf16[128,640]{1,0:T(8,128)(2,1)S(1)}, u32[]{:S(2)}, u32[]{:S(2)}) collective-permute-start(bf16[128,640]{1,0:T(8,128)(2,1)S(1)} %copy-done.54), channel_id=1, source_target_pairs={{0,1},{1,0},{2,3},{3,2},{4,5},{5,4},{6,7},{7,6},{8,9},{9,8},{10,11... | collective-permute-start | bytes 491528 | tf_op jit(solution)/shard_map/ppermute | solution.py:66
  210.9 102.9 %copy-start.67 = (f32[128]{0:T(128)S(1)}, f32[128]{0:T(128)}, u32[]{:S(2)}) copy-start(f32[128]{0:T(128)} %copy-done.66) | copy-start | bytes 1540
  210.9 102.9 %copy-start.69 = (f32[128]{0:T(128)S(1)}, f32[128]{0:T(128)}, u32[]{:S(2)}) copy-start(f32[128]{0:T(128)} %copy-done.68) | copy-start | bytes 1540
  210.9 103.3 %copy-start.18 = (f32[128,256]{1,0:T(8,128)S(1)}, f32[128,256]{1,0:T(8,128)}, u32[]{:S(2)}) copy-start(f32[128,256]{1,0:T(8,128)} %copy-done.17) | copy-start | bytes 393220
  210.9 103.3 %copy-start.62 = (f32[128]{0:T(128)S(1)}, f32[128]{0:T(128)}, u32[]{:S(2)}) copy-start(f32[128]{0:T(128)} %copy-done.61) | copy-start | bytes 1540
  211.0 103.5 %copy-start.47 = (bf16[640,128]{1,0:T(8,128)(2,1)S(1)}, bf16[640,128]{1,0:T(8,128)(2,1)}, u32[]{:S(2)}) copy-start(bf16[640,128]{1,0:T(8,128)(2,1)} %param.20) | copy-start | bytes 491524
  211.0 103.5 %copy-start.52 = (bf16[640,128]{1,0:T(8,128)(2,1)S(1)}, bf16[640,128]{1,0:T(8,128)(2,1)}, u32[]{:S(2)}) copy-start(bf16[640,128]{1,0:T(8,128)(2,1)} %copy-done.51) | copy-start | bytes 491524
  211.0 103.8 %copy-start.48 = (bf16[640,128]{1,0:T(8,128)(2,1)S(1)}, bf16[640,128]{1,0:T(8,128)(2,1)}, u32[]{:S(2)}) copy-start(bf16[640,128]{1,0:T(8,128)(2,1)} %param.21) | copy-start | bytes 491524
  211.0 103.8 %copy-start.50 = (bf16[640,128]{1,0:T(8,128)(2,1)S(1)}, bf16[640,128]{1,0:T(8,128)(2,1)}, u32[]{:S(2)}) copy-start(bf16[640,128]{1,0:T(8,128)(2,1)} %copy-done.49) | copy-start | bytes 491524
  211.0 103.8 %copy-start.65 = (f32[128]{0:T(128)S(1)}, f32[128]{0:T(128)}, u32[]{:S(2)}) copy-start(f32[128]{0:T(128)} %copy-done.64) | copy-start | bytes 1540
  315.4 1.2 collective-permute-start.10
  315.5 1.5 collective-permute-start.9
  319.9 119.3 %all-to-all-start.1 = ((bf16[64,2,1300]{2,1,0:T(2,128)(2,1)}), bf16[64,2,1300]{2,1,0:T(2,128)(2,1)S(1)}, u32[]{:S(2)}, u32[]{:S(2)}) async-start(bf16[64,2,1300]{2,1,0:T(2,128)(2,1)} %reshape.477), calls=%async_computation.1 | async-start | bytes 720896 | tf_op jit(solution)/shard_map/all_to_all | solution.py:102
  444.6 19.3 %all-to-all-start.2 = ((bf16[64,2,1300]{2,1,0:T(2,128)(2,1)}), bf16[64,2,1300]{2,1,0:T(2,128)(2,1)S(1)}, u32[]{:S(2)}, u32[]{:S(2)}) async-start(bf16[64,2,1300]{2,1,0:T(2,128)(2,1)} %reshape.479), calls=%async_computation.2 | async-start | bytes 720896 | tf_op jit(solution)/shard_map/all_to_all | solution.py:105
  (67 other events, 717.4 us)
Sparse Core Ops, SparseCore 0:
  20.7 81.1 all-gather.1
  208.0 221.1 all-reduce.3
where the time goes:
time: 485 us; the launch traced here: 477 us
  waiting for transfers between devices  285 us (59%)
  matrix products  82.5 us (17%)
  other arithmetic  42.9 us (9%)
  starting transfers between devices  30.8 us (6%)
  local copies, waits for them, and re-layouts  19.3 us (4%)
  between operations  15.9 us (3%)
    psum x1, waiting for transfers between devices, per_device(): lax.psum(big, CTX)  101 us
    all_to_all x1, waiting for transfers between devices, scatter_sum(): lax.all_to_all(parts.reshape(64, 128, -1), CTX, split_axis=0, concat_axis...  97.9 us
    all_gather x1, waiting for transfers between devices, gather_ctx(): return lax.all_gather(block, CTX, axis=0, tiled=True)  75.5 us
    dot_general x14, matrix products, dot_nt(): lax.dot_general(left, right, (((1,), (1,)), ((), ())), preferred_element_...  35.6 us
    dot_general x14, matrix products, dot_f32(): return jnp.dot(left, right, preferred_element_type=f32)  31.8 us
    dot_general x8, matrix products, dot_tn(): lax.dot_general(left, right, (((0,), (0,)), ((), ())), preferred_element_...  15.1 us
    all_to_all x1, waiting for transfers between devices, small_sum(): out = lax.all_to_all(wide, CTX, split_axis=0, concat_axis=0, tiled=True)  10.7 us
    convert_element_type x5, other arithmetic, per_device(): g.astype(f32)  9.98 us
  transfers between devices with their start and end apart: 23, of which 6 were waited for; matrix products, arithmetic and copies ran while one was open for 18% of the time, Pallas kernels for 0%

commit v1 on v0

--- a/solution.py
+++ b/solution.py
@@ -243,7 +243,9 @@
     big = tuple(
         (g.astype(bf16) for g in (grad_w_query, grad_w_out, grad_w_gate, grad_w_up, grad_w_down))
     )
-    sum_query, sum_out, sum_gate, sum_up, sum_down = (g.astype(f32) for g in lax.psum(big, CTX))
+    sum_query, sum_out, sum_gate, sum_up, sum_down = (
+        g.astype(f32) for g in lax.psum(lax.psum(big, "z"), ("x", "y"))
+    )
     kv_mine = scatter_sum(kv_terms)
     grad_key_raw, grad_gain_key = rms_backward(
         key_raw, key_factor, gain_key, rotate_back(kv_mine[:, :HDIM], cos_tab, sin_tab)

time: 485 us -> 533 us (1.099)
  waiting for transfers between devices: 285 us -> 321 us
  blocking collectives: 0 us -> 24.9 us
  starting transfers between devices: 30.8 us -> 19.1 us
    psum x1 -> x2, waiting for transfers between devices: 101 us -> 234 us  [the longest x1 176 us: per_device(): lax.psum(big, 'z')]
    all_to_all x1, waiting for transfers between devices: 97.9 us -> 0.01 us  [scatter_sum(): lax.all_to_all(parts.reshape(64, 128, -1), CTX, split_axis=0, concat_axis...]
    all_to_all x0 -> x1, blocking collectives: none -> 24.9 us  [small_sum(): lax.all_to_all(values.reshape(64, rows, -1), CTX, split_axis=0, concat_ax...]
    all_to_all x1 -> x0, starting transfers between devices: 8.71 us -> none  [small_sum(): lax.all_to_all(values.reshape(64, rows, -1), CTX, split_axis=0, concat_ax...]
  transfers between devices with their start and end apart: 23 -> 23, of which waited for: 6 -> 6; matrix products, arithmetic and copies ran while one was open for 18% -> 16% of each run, Pallas kernels for 0% -> 0%
where the time goes in v1:
time: 533 us; the launch traced here: 524 us
  waiting for transfers between devices  321 us (60%)
  matrix products  82.5 us (15%)
  other arithmetic  43 us (8%)
  blocking collectives  24.9 us (5%)
  starting transfers between devices  19.1 us (4%)
  local copies, waits for them, and re-layouts  18.6 us (3%)
  between operations  15.6 us (3%)
    psum x1, waiting for transfers between devices, per_device(): lax.psum(big, 'z')  176 us
    all_gather x1, waiting for transfers between devices, gather_ctx(): return lax.all_gather(block, CTX, axis=0, tiled=True)  75.5 us
    psum x1, waiting for transfers between devices, per_device(): lax.psum(lax.psum(big, 'z'), ('x', 'y'))  58.5 us
    dot_general x14, matrix products, dot_nt(): lax.dot_general(left, right, (((1,), (1,)), ((), ())), preferred_element_...  35.6 us
    dot_general x14, matrix products, dot_f32(): return jnp.dot(left, right, preferred_element_type=f32)  31.8 us
    all_to_all x1, blocking collectives, small_sum(): lax.all_to_all(values.reshape(64, rows, -1), CTX, split_axis=0, concat_ax...  24.9 us
    dot_general x8, matrix products, dot_tn(): lax.dot_general(left, right, (((0,), (0,)), ((), ())), preferred_element_...  15.1 us
  transfers between devices with their start and end apart: 23, of which 6 were waited for; matrix products, arithmetic and copies ran while one was open for 16% of the time, Pallas kernels for 0%

profile of v1, /device:TPU:0, one launch (start us, length us, event | category | flops | bytes accessed | tf_op | source)
XLA Modules:
  0.0 524.4 jit_solution(12488105035314445632)
XLA Ops:
  7.2 4.3 concatenate.211
  26.4 75.5 %all-gather.2.cloned.1.call-done = bf16[8192,512]{1,0:T(8,128)(2,1)} async-done(((bf16[128,512]{1,0:T(8,128)(2,1)}), bf16[8192,512]{1,0:T(8,128)(2,1)}) %all-gather.2.cloned.1.call-update) | async-done | bytes 8388624 | tf_op jit(solution)/shard_map/all_gather | solution.py:92
  101.9 10.8 %fusion.133 = (f32[512]{0:T(512)S(1)}, f32[512,8192]{1,0:T(8,128)}) fusion(bf16[8192,512]{1,0:T(8,128)(2,1)} %all-gather.2.cloned.1.call-done, bf16[512,128]{1,0:T(8,128)(2,1)} %get-tuple-element.104, bf16[512,128]{1,0:T(8,128)(2,1)S(1)} %get-tuple-element.103, s32[512]{0:T(512)S(1)} %broadcast_bitcast_fusion, s32[8192]{0:T(1024)S(1)} %add.257), kind=kOutput, calls=%fused_computation.278 | convolution fusion | flops 2164784640 | bytes 21270528 | tf_op jit(solution)/shard_map/dot_general | solution.py:58
  112.8 8.1 %fusion = f32[512]{0:T(512)S(1)} fusion(f32[512,8192]{1,0:T(8,128)} %get-tuple-element.164, f32[512]{0:T(512)S(1)} %get-tuple-element.163), kind=kLoop, calls=%fused_computation.6 | loop fusion | flops 8388096 | bytes 16781312 | tf_op jit(solution)/shard_map/reduce_sum | solution.py:74
  120.9 10.0 %fusion.14 = bf16[512,256]{0,1:T(8,128)(2,1)S(1)} fusion(bf16[8192,512]{1,0:T(8,128)(2,1)} %all-gather.2.cloned.1.call-done, f32[512,8192]{1,0:T(8,128)} %get-tuple-element.164, f32[512]{0:T(512)S(1)} %fusion, f32[512]{0:T(512)S(1)} %get-tuple-element.163), kind=kOutput, calls=%fused_computation.27 | convolution fusion | flops 2160197632 | bytes 21237760 | tf_op jit(solution)/shard_map/dot_general | solution.py:54
  134.4 1.7 fusion.136
  137.0 1.8 fusion.138
  139.3 1.9 multiply_reduce_fusion.9
  143.6 2.0 fusion.139
  145.7 2.2 multiply_convert_fusion.2
  147.9 2.1 convolution_add_fusion.5
  156.1 5.2 convolution_convert_fusion
  161.3 10.0 %multiply_convert_fusion = bf16[512,8192]{1,0:T(8,128)(2,1)S(1)} fusion(f32[512,8192]{1,0:T(8,128)} %get-tuple-element.164, f32[512]{0:T(512)S(1)} %multiply_reduce_fusion.2, f32[512]{0:T(512)S(1)} %log_add_fusion, bf16[8192,512]{1,0:T(8,128)(2,1)} %all-gather.2.cloned.1.call-done, bf16[128,256]{0,1:T(8,128)(2,1)S(1)} %get-tuple-element.136, ...), kind=kOutput, calls=%fused_computation.1 | convolution fusion | flops 2165309440 | bytes 29626368 | tf_op jit(solution)/shard_map/dot_general | solution.py:58
  171.3 2.4 fusion.2
  173.7 1.8 copy-done.1
  176.6 4.4 copy_bitcast_fusion
  181.0 9.0 %all-to-all-start = ((bf16[64,128,512]{1,2,0:T(8,128)(2,1)}), bf16[64,128,512]{1,2,0:T(8,128)(2,1)}, u32[]{:S(2)}, u32[]{:S(2)}) async-start(bf16[64,128,512]{1,2,0:T(8,128)(2,1)} %copy_bitcast_fusion), calls=%async_computation | async-start | bytes 16777216 | tf_op jit(solution)/shard_map/all_to_all | solution.py:96
  190.2 6.9 %fusion.11 = f32[512,256]{1,0:T(8,128)S(1)} fusion(bf16[512,8192]{1,0:T(8,128)(2,1)} %copy-done.1, bf16[8192,512]{1,0:T(8,128)(2,1)} %all-gather.2.cloned.1.call-done), kind=kOutput, calls=%fused_computation.26 | convolution fusion | flops 2147614720 | bytes 13107200 | tf_op jit(solution)/shard_map/dot_general | solution.py:54
  203.0 1.6 convolution_convert_fusion.3
  206.2 1.7 convolution_convert_fusion.1
  211.0 175.8 %all-reduce.8.cloned.1.call-done = (bf16[640,512]{1,0:T(8,128)(2,1)}, bf16[512,640]{1,0:T(8,128)(2,1)}, bf16[640,1024]{1,0:T(8,128)(2,1)}, bf16[640,1024]{1,0:T(8,128)(2,1)}, bf16[1024,640]{1,0:T(8,128)(2,1)}) async-done(((bf16[640,512]{1,0:T(8,128)(2,1)}, bf16[512,640]{1,0:T(8,128)(2,1)}, bf16[640,1024]{1,0:T(8,128)(2,1)}, bf16[640,1024]{1,0:T(8,128)(2,1)}, bf16[1024,640]{1,0:T(8,128)(2,1)}), ...) | async-done | bytes 5242896 | tf_op jit(solution)/shard_map/psum | solution.py:247
  386.9 4.8 convert_reduce_fusion
  397.2 24.9 %all_to_all.15 = bf16[64,2,1300]{2,1,0:T(2,128)(2,1)S(1)} all-to-all(bf16[64,2,1300]{2,1,0:T(2,128)(2,1)S(1)} %reshape.477), channel_id=1, replica_groups=mesh['z'=4,'x'=4,'y'=4,'wsh'=2] {'z','x','y'}, dimensions={0} | all-to-all | bytes 665600 | tf_op jit(solution)/shard_map/all_to_all | solution.py:102
  423.6 2.8 reduce.22
  427.5 4.7 all-to-all-start.2
  433.1 10.2 %all-to-all-done.2 = bf16[64,2,1300]{2,1,0:T(2,128)(2,1)S(1)} async-done(((bf16[64,2,1300]{2,1,0:T(2,128)(2,1)}), bf16[64,2,1300]{2,1,0:T(2,128)(2,1)S(1)}, u32[]{:S(2)}, u32[]{:S(2)}) %all-to-all-start.2) | async-done | bytes 332832 | tf_op jit(solution)/shard_map/all_to_all | solution.py:105
  449.2 58.5 %all-reduce.6.cloned.1.call-done = (bf16[640,512]{1,0:T(8,128)(2,1)}, bf16[512,640]{1,0:T(8,128)(2,1)}, bf16[640,1024]{1,0:T(8,128)(2,1)}, bf16[640,1024]{1,0:T(8,128)(2,1)}, bf16[1024,640]{1,0:T(8,128)(2,1)}) async-done(((bf16[640,512]{1,0:T(8,128)(2,1)}, bf16[512,640]{1,0:T(8,128)(2,1)}, bf16[640,1024]{1,0:T(8,128)(2,1)}, bf16[640,1024]{1,0:T(8,128)(2,1)}, bf16[1024,640]{1,0:T(8,128)(2,1)}), ...) | async-done | bytes 5242896 | tf_op jit(solution)/shard_map/psum | solution.py:247
  507.7 2.5 convert_element_type.209
  510.2 2.2 convert_element_type.215
  512.4 1.8 convert_element_type.217
  514.2 1.8 convert_element_type.219
  516.0 1.7 convert_element_type.221
  (325 shorter events, 53.6 us)
Async XLA Ops:
  7.2 14.7 %copy-start.63 = (s32[64,2]{0,1:T(2,128)S(1)}, s32[64,2]{0,1:T(2,128)}, u32[]{:S(2)}) copy-start(s32[64,2]{0,1:T(2,128)} %param.18) | copy-start | bytes 1540
  7.2 14.2 %copy-start.2 = (bf16[640,1024]{1,0:T(8,128)(2,1)S(1)}, bf16[640,1024]{1,0:T(8,128)(2,1)}, u32[]{:S(2)}) copy-start(bf16[640,1024]{1,0:T(8,128)(2,1)} %param.24) | copy-start | bytes 3932164
  7.2 94.7 %all-gather.2.cloned.1.call-start = ((), (), s32[]{:S(2)}) async-start(), calls=%async_computation.3 | async-start | bytes 8519680 | tf_op jit(solution)/shard_map/all_gather | solution.py:92
  11.5 3.9 collective-permute-start
  12.7 4.0 collective-permute-start.2
  19.9 92.9 %copy-start.27 = (f32[128,128]{1,0:T(8,128)}, f32[128,128]{1,0:T(8,128)S(1)}, u32[]{:S(2)}) copy-start(f32[128,128]{1,0:T(8,128)S(1)} %get-tuple-element.157) | copy-start | bytes 196612
  19.9 92.9 %copy-start.29 = (f32[128,128]{1,0:T(8,128)}, f32[128,128]{1,0:T(8,128)S(1)}, u32[]{:S(2)}) copy-start(f32[128,128]{1,0:T(8,128)S(1)} %get-tuple-element.158) | copy-start | bytes 196612
  20.6 3.4 collective-permute-start.1
  20.7 111.9 %collective-permute-start.3 = (bf16[512,640]{1,0:T(8,128)(2,1)}, bf16[512,640]{1,0:T(8,128)(2,1)}, u32[]{:S(2)}, u32[]{:S(2)}) collective-permute-start(bf16[512,640]{1,0:T(8,128)(2,1)} %param.22), channel_id=1, source_target_pairs={{0,1},{1,0},{2,3},{3,2},{4,5},{5,4},{6,7},{7,6},{8,9},{9,8},{10,11... | collective-permute-start | bytes 1966088 | tf_op jit(solution)/shard_map/ppermute | solution.py:66
  21.2 115.8 %collective-permute-start.4 = (bf16[640,1024]{1,0:T(8,128)(2,1)}, bf16[640,1024]{1,0:T(8,128)(2,1)}, u32[]{:S(2)}, u32[]{:S(2)}) collective-permute-start(bf16[640,1024]{1,0:T(8,128)(2,1)} %param.23), channel_id=1, source_target_pairs={{0,1},{1,0},{2,3},{3,2},{4,5},{5,4},{6,7},{7,6},{8,9},{9,8},{10,11... | collective-permute-start | bytes 3932168 | tf_op jit(solution)/shard_map/ppermute | solution.py:66
  21.4 117.5 %collective-permute-start.5 = (bf16[640,1024]{1,0:T(8,128)(2,1)S(1)}, bf16[640,1024]{1,0:T(8,128)(2,1)S(1)}, u32[]{:S(2)}, u32[]{:S(2)}) collective-permute-start(bf16[640,1024]{1,0:T(8,128)(2,1)S(1)} %copy-done.2), channel_id=1, source_target_pairs={{0,1},{1,0},{2,3},{3,2},{4,5},{5,4},{6,7},{7,6},{8,9},{9,8},{10,11... | collective-permute-start | bytes 3932168 | tf_op jit(solution)/shard_map/ppermute | solution.py:66
  21.8 117.5 %collective-permute-start.6 = (bf16[1024,640]{1,0:T(8,128)(2,1)}, bf16[1024,640]{1,0:T(8,128)(2,1)}, u32[]{:S(2)}, u32[]{:S(2)}) collective-permute-start(bf16[1024,640]{1,0:T(8,128)(2,1)} %param.25), channel_id=1, source_target_pairs={{0,1},{1,0},{2,3},{3,2},{4,5},{5,4},{6,7},{7,6},{8,9},{9,8},{10,11... | collective-permute-start | bytes 3932168 | tf_op jit(solution)/shard_map/ppermute | solution.py:66
  22.5 90.3 %copy-start.59 = (f32[256]{0:T(256)}, f32[256]{0:T(256)S(1)}, u32[]{:S(2)}) copy-start(f32[256]{0:T(256)S(1)} %convert_add_fusion.6) | copy-start | bytes 3076
  26.4 86.4 %copy-start.55 = (bf16[512,128]{1,0:T(8,128)(2,1)}, bf16[512,128]{1,0:T(8,128)(2,1)S(1)}, u32[]{:S(2)}) copy-start(bf16[512,128]{1,0:T(8,128)(2,1)S(1)} %get-tuple-element.103) | copy-start | bytes 393220
  137.0 19.1 %slice-start = ((s8[16777216]{0:T(1024)(128)(4,1)}), s8[4194304]{0:T(1024)(128)(4,1)S(1)}, s32[]{:S(2)}) async-start(s8[16777216]{0:T(1024)(128)(4,1)} %bitcast.111), calls=%async_computation.6 | async-start | bytes 8388608
  141.9 14.2 %slice-start.1 = ((s8[16777216]{0:T(1024)(128)(4,1)}), s8[4194304]{0:T(1024)(128)(4,1)S(1)}, s32[]{:S(2)}) async-start(s8[16777216]{0:T(1024)(128)(4,1)} %bitcast.111), calls=%async_computation.7 | async-start | bytes 8388608
  181.0 205.9 %all-to-all-start = ((bf16[64,128,512]{1,2,0:T(8,128)(2,1)}), bf16[64,128,512]{1,2,0:T(8,128)(2,1)}, u32[]{:S(2)}, u32[]{:S(2)}) async-start(bf16[64,128,512]{1,2,0:T(8,128)(2,1)} %copy_bitcast_fusion), calls=%async_computation | async-start | bytes 16777216 | tf_op jit(solution)/shard_map/all_to_all | solution.py:96
  190.0 196.7 %all-reduce.8.cloned.1.call-start = ((), (), s32[]{:S(2)}) async-start(), calls=%async_computation.5 | async-start | bytes 10485760 | tf_op jit(solution)/shard_map/psum | solution.py:247
  190.1 9.1 %collective-permute-start.7 = (bf16[128,640]{1,0:T(8,128)(2,1)S(1)}, bf16[128,640]{1,0:T(8,128)(2,1)S(1)}, u32[]{:S(2)}, u32[]{:S(2)}) collective-permute-start(bf16[128,640]{1,0:T(8,128)(2,1)S(1)} %copy-done.10), channel_id=1, source_target_pairs={{0,1},{1,0},{2,3},{3,2},{4,5},{5,4},{6,7},{7,6},{8,9},{9,8},{10,11... | collective-permute-start | bytes 491528 | tf_op jit(solution)/shard_map/ppermute | solution.py:66
  197.9 1.7 collective-permute-start.8
  198.5 2.9 collective-permute-start.12
  198.6 4.4 collective-permute-start.14
  199.0 2.0 collective-permute-start.11
  199.2 3.8 collective-permute-start.13
  199.6 4.9 collective-permute-start.15
  201.1 5.1 collective-permute-start.16
  201.4 4.8 collective-permute-start.17
  207.9 299.8 %all-reduce.6.cloned.1.call-start = ((), (), s32[]{:S(2)}) async-start(), calls=%async_computation.4 | async-start | bytes 10485760 | tf_op jit(solution)/shard_map/psum | solution.py:247
  393.4 1.2 collective-permute-start.10
  393.5 1.5 collective-permute-start.9
  395.3 36.9 %copy-start.7 = (f32[128,640]{1,0:T(8,128)S(1)}, f32[128,640]{1,0:T(8,128)}, u32[]{:S(2)}) copy-start(f32[128,640]{1,0:T(8,128)} %copy-done.6) | copy-start | bytes 983044
  427.5 15.8 %all-to-all-start.2 = ((bf16[64,2,1300]{2,1,0:T(2,128)(2,1)}), bf16[64,2,1300]{2,1,0:T(2,128)(2,1)S(1)}, u32[]{:S(2)}, u32[]{:S(2)}) async-start(bf16[64,2,1300]{2,1,0:T(2,128)(2,1)} %reshape.479), calls=%async_computation.2 | async-start | bytes 720896 | tf_op jit(solution)/shard_map/all_to_all | solution.py:105
  (67 other events, 328.4 us)
Sparse Core Ops, SparseCore 0:
  20.7 81.1 all-gather.1
  208.0 178.6 all-reduce.7
  390.6 117.0 all-reduce.5
